TPU v7x, 32 devices: a whole 2x2x4 slice. The times are simulated.
32 devices in a mesh: wide: 8 (over z, x), narrow: 4 (over y, core).
Axes of the slice: x: 2, y: 2, z: 4, core: 2. Of those that a mesh axis runs over, the one named last changes fastest.
Arguments:
- tokens: bfloat16 [64, 512, 768], P(('wide', 'narrow')), may hold values from -6 to 6
- doc_lengths: int32 [64], P(('wide', 'narrow')), may hold values from 30 to 512
- qkv_weight: bfloat16 [768, 2304], replicated, may hold values from -0.21875 to 0.21875
- query_bias: bfloat16 [768], replicated, may hold values from -3 to 3
- value_bias: bfloat16 [768], replicated, may hold values from -3 to 3
- out_weight: bfloat16 [768, 768], replicated, may hold values from -0.625 to 0.625
- out_bias: bfloat16 [768], replicated, may hold values from -1.75 to 1.75
- first_gain: bfloat16 [768], replicated, may hold values from 0.5 to 1.5
- first_shift: bfloat16 [768], replicated, may hold values from -1.75 to 1.75
- up_weight: bfloat16 [768, 3072], replicated, may hold values from -0.21875 to 0.21875
- up_bias: bfloat16 [3072], replicated, may hold values from -3 to 3
- down_weight: bfloat16 [3072, 768], replicated, may hold values from -0.15625 to 0.15625
- down_bias: bfloat16 [768], replicated, may hold values from -1.75 to 1.75
- second_gain: bfloat16 [768], replicated, may hold values from 0.5 to 1.5
- second_shift: bfloat16 [768], replicated, may hold values from -1.75 to 1.75
- dir_weight: bfloat16 [1536, 8], replicated, may hold values from -0.375 to 0.375
- dir_bias: bfloat16 [8], replicated, may hold values from -1 to 1
- segment_rows: int32 [64, 128], P(('wide', 'narrow')), may hold values from 0 to 511, as said below
- segment_slots: int32 [32, 256], P(('wide', 'narrow')), may hold values from 0 to 255, each once within a row
- pair_rows: int32 [32, 256, 2], P(('wide', 'narrow')), may hold values from 0 to 255
- pair_labels: int32 [32, 256], P(('wide', 'narrow')), may hold values from 0 to 7
- out_cotangent: bfloat16 [64, 512, 768], P(('wide', 'narrow')), may hold values from -6 to 6
Outputs:
- encoded: bfloat16 [64, 512, 768], P(('wide', 'narrow'))
- grad_tokens: bfloat16 [64, 512, 768], P(('wide', 'narrow'))
- grad_qkv_weight: float32 [768, 2304], P('narrow', 'wide')
- grad_query_bias: float32 [768], replicated
- grad_value_bias: float32 [768], replicated
- grad_out_weight: float32 [768, 768], P('narrow', 'wide')
- grad_out_bias: float32 [768], replicated
- grad_first_gain: float32 [768], replicated
- grad_first_shift: float32 [768], replicated
- grad_up_weight: float32 [768, 3072], P('narrow', 'wide')
- grad_up_bias: float32 [3072], replicated
- grad_down_weight: float32 [3072, 768], P('narrow', 'wide')
- grad_down_bias: float32 [768], replicated
- grad_second_gain: float32 [768], replicated
- grad_second_shift: float32 [768], replicated
- grad_dir_weight: float32 [1536, 8], replicated
- grad_dir_bias: float32 [8], replicated
Inputs may be any that keep to these rules, and one draw needn't show every extreme that they name: `segment_rows`: each value is below the token count of its document. `segment_slots`: each device's row holds every slot once.
All inputs are finite; a program needn't handle non-finite values.
Results may differ from a plain program's by a relative error of at most 0.02.
Values may be sent and summed in bfloat16 or wider, within the bound.
A program may use at most 192 MiB of HBM per device.

v0:
```python
import jax
import jax.numpy as jnp
from jax import lax
from jax.sharding import PartitionSpec as P

HEADS = 12
HEAD_DIM = 64


EXACT = lax.Precision.HIGHEST
MASKED = -1e30
EPSILON = 1e-05


def norm_forward(values, gain, shift):
    center = jnp.mean(values, -1, keepdims=True)
    centered = values - center
    inverse = lax.rsqrt(jnp.mean(centered * centered, -1, keepdims=True) + EPSILON)
    normed = centered * inverse
    return (normed * gain + shift, normed, inverse)


def norm_backward(grad, normed, inverse, gain):
    scaled = grad * gain
    first_mean = jnp.mean(scaled, -1, keepdims=True)
    second_mean = jnp.mean(scaled * normed, -1, keepdims=True)
    return (
        (scaled - first_mean - normed * second_mean) * inverse,
        jnp.sum(grad * normed, 0),
        jnp.sum(grad, 0),
    )


def normal_cdf(values):
    return 0.5 * (1.0 + lax.erf(values * 0.7071067811865476))


def on_device(
    tokens,
    doc_lengths,
    qkv_weight,
    query_bias,
    value_bias,
    out_weight,
    out_bias,
    first_gain,
    first_shift,
    up_weight,
    up_bias,
    down_weight,
    down_bias,
    second_gain,
    second_shift,
    dir_weight,
    dir_bias,
    segment_rows,
    segment_slots,
    pair_rows,
    pair_labels,
    out_cotangent,
):
    doc_count, length, model_width = tokens.shape
    score_scale = HEAD_DIM ** (-0.5)
    token_rows = tokens.reshape(doc_count * length, model_width)
    allowed = lax.broadcasted_iota(jnp.int32, (doc_count, length), 1) < doc_lengths[:, None]
    allowed_rows = allowed.reshape(-1, 1).astype(jnp.float32)
    bias_row = jnp.concatenate([query_bias, jnp.zeros_like(query_bias), value_bias]).astype(
        jnp.float32
    )
    qkv = (jnp.dot(token_rows, qkv_weight, preferred_element_type=jnp.float32) + bias_row).astype(
        jnp.bfloat16
    )

    def split_heads(doc_block, which):
        return doc_block[:, which * model_width : (which + 1) * model_width].reshape(
            length, HEADS, HEAD_DIM
        )

    def scores_of(queries, key_rows, doc_mask):
        scores = (
            jnp.einsum("qhd,khd->hqk", queries, key_rows, preferred_element_type=jnp.float32)
            * score_scale
        )
        return jnp.where(doc_mask[None, None, :], scores, MASKED)

    mixed_parts = []
    log_totals = []
    for doc_index in range(doc_count):
        doc_block = qkv[doc_index * length : (doc_index + 1) * length]
        queries = split_heads(doc_block, 0)
        key_rows = split_heads(doc_block, 1)
        value_rows = split_heads(doc_block, 2)
        scores = scores_of(queries, key_rows, allowed[doc_index])
        highest = jnp.max(scores, -1, keepdims=True)
        powers = jnp.exp(scores - highest)
        summed = jnp.sum(powers, -1, keepdims=True)
        attention = (powers / summed).astype(jnp.bfloat16)
        log_totals.append(highest + jnp.log(summed))
        mixed_parts.append(
            jnp.einsum(
                "hqk,khd->qhd", attention, value_rows, preferred_element_type=jnp.float32
            ).reshape(length, model_width)
        )
    mixed = jnp.concatenate(mixed_parts).astype(jnp.bfloat16)
    attended = jnp.dot(mixed, out_weight, preferred_element_type=jnp.float32) + out_bias.astype(
        jnp.float32
    )
    resid_one = token_rows.astype(jnp.float32) + attended
    hidden_one, normed_one, inverse_one = norm_forward(
        resid_one, first_gain.astype(jnp.float32), first_shift.astype(jnp.float32)
    )
    hidden_low = hidden_one.astype(jnp.bfloat16)
    upper_pre = jnp.dot(hidden_low, up_weight, preferred_element_type=jnp.float32) + up_bias.astype(
        jnp.float32
    )
    cumulative = normal_cdf(upper_pre)
    active = (upper_pre * cumulative).astype(jnp.bfloat16)
    lowered = jnp.dot(active, down_weight, preferred_element_type=jnp.float32) + down_bias.astype(
        jnp.float32
    )
    resid_two = hidden_one + lowered
    second_float = second_gain.astype(jnp.float32)
    normed_out, normed_two, inverse_two = norm_forward(
        resid_two, second_float, second_shift.astype(jnp.float32)
    )
    encoded_rows = (normed_out * allowed_rows).astype(jnp.bfloat16)
    doc_starts = lax.broadcasted_iota(jnp.int32, (doc_count, 1), 0) * length
    picked_rows = (segment_rows + doc_starts).reshape(-1)
    picked = encoded_rows[picked_rows]
    slots = segment_slots.reshape(-1)
    outgoing = jnp.zeros_like(picked).at[slots].set(picked)
    arrived = lax.all_to_all(outgoing, "wide", split_axis=0, concat_axis=0, tiled=True)
    pairs = pair_rows.reshape(-1, 2)
    labels = pair_labels.reshape(-1)
    first_rows = arrived[pairs[:, 0]]
    second_rows = arrived[pairs[:, 1]]
    logits = (
        jnp.dot(first_rows, dir_weight[:model_width], preferred_element_type=jnp.float32)
        + jnp.dot(second_rows, dir_weight[model_width:], preferred_element_type=jnp.float32)
        + dir_bias.astype(jnp.float32)
    )
    powers_head = jnp.exp(logits - jnp.max(logits, -1, keepdims=True))
    chance = powers_head / jnp.sum(powers_head, -1, keepdims=True)
    classes = lax.broadcasted_iota(jnp.int32, logits.shape, 1)
    delta = chance - (labels[:, None] == classes).astype(jnp.float32)
    first_float = first_rows.astype(jnp.float32)
    second_rows_float = second_rows.astype(jnp.float32)
    grad_dir_weight = jnp.concatenate(
        [
            jnp.dot(first_float.T, delta, precision=EXACT, preferred_element_type=jnp.float32),
            jnp.dot(
                second_rows_float.T, delta, precision=EXACT, preferred_element_type=jnp.float32
            ),
        ]
    )
    grad_dir_bias = jnp.sum(delta, 0)
    dir_float = dir_weight.astype(jnp.float32)
    grad_first = jnp.dot(
        delta, dir_float[:model_width].T, precision=EXACT, preferred_element_type=jnp.float32
    )
    grad_second = jnp.dot(
        delta, dir_float[model_width:].T, precision=EXACT, preferred_element_type=jnp.float32
    )
    grad_arrived = jnp.zeros((arrived.shape[0], model_width), jnp.float32)
    grad_arrived = grad_arrived.at[pairs[:, 0]].add(grad_first).at[pairs[:, 1]].add(grad_second)
    returned = lax.all_to_all(
        grad_arrived.astype(jnp.bfloat16), "wide", split_axis=0, concat_axis=0, tiled=True
    )
    grad_picked = returned[slots].astype(jnp.float32)
    grad_encoded = (
        out_cotangent.reshape(-1, model_width).astype(jnp.float32).at[picked_rows].add(grad_picked)
    )
    grad_encoded = grad_encoded * allowed_rows
    grad_two, grad_second_gain, grad_second_shift = norm_backward(
        grad_encoded, normed_two, inverse_two, second_float
    )
    grad_lowered = grad_two.astype(jnp.bfloat16)
    grad_down_weight = jnp.einsum(
        "rf,rd->fd", active, grad_lowered, preferred_element_type=jnp.float32
    )
    grad_down_bias = jnp.sum(grad_lowered.astype(jnp.float32), 0)
    grad_active = jnp.einsum(
        "rd,fd->rf", grad_lowered, down_weight, preferred_element_type=jnp.float32
    )
    density = jnp.exp(-0.5 * upper_pre * upper_pre) * 0.3989422804014327
    grad_upper = (grad_active * (cumulative + upper_pre * density)).astype(jnp.bfloat16)
    grad_up_weight = jnp.einsum(
        "rd,rf->df", hidden_low, grad_upper, preferred_element_type=jnp.float32
    )
    grad_up_bias = jnp.sum(grad_upper.astype(jnp.float32), 0)
    grad_hidden = grad_two + jnp.einsum(
        "rf,df->rd", grad_upper, up_weight, preferred_element_type=jnp.float32
    )
    grad_one, grad_first_gain, grad_first_shift = norm_backward(
        grad_hidden, normed_one, inverse_one, first_gain.astype(jnp.float32)
    )
    grad_attended = grad_one.astype(jnp.bfloat16)
    grad_out_weight = jnp.einsum(
        "rd,re->de", mixed, grad_attended, preferred_element_type=jnp.float32
    )
    grad_out_bias = jnp.sum(grad_attended.astype(jnp.float32), 0)
    grad_mixed = jnp.einsum(
        "re,de->rd", grad_attended, out_weight, preferred_element_type=jnp.float32
    ).astype(jnp.bfloat16)
    grad_parts = []
    for doc_index in range(doc_count):
        doc_block = qkv[doc_index * length : (doc_index + 1) * length]
        queries = split_heads(doc_block, 0)
        key_rows = split_heads(doc_block, 1)
        value_rows = split_heads(doc_block, 2)
        scores = scores_of(queries, key_rows, allowed[doc_index])
        attention = jnp.exp(scores - log_totals[doc_index])
        grad_doc = grad_mixed[doc_index * length : (doc_index + 1) * length].reshape(
            length, HEADS, HEAD_DIM
        )
        grad_chance = jnp.einsum(
            "qhd,khd->hqk", grad_doc, value_rows, preferred_element_type=jnp.float32
        )
        inner = jnp.sum(grad_chance * attention, -1, keepdims=True)
        grad_scores = (attention * (grad_chance - inner)).astype(jnp.bfloat16)
        grad_query = (
            jnp.einsum("hqk,khd->qhd", grad_scores, key_rows, preferred_element_type=jnp.float32)
            * score_scale
        )
        grad_key = (
            jnp.einsum("hqk,qhd->khd", grad_scores, queries, preferred_element_type=jnp.float32)
            * score_scale
        )
        grad_value = jnp.einsum(
            "hqk,qhd->khd",
            attention.astype(jnp.bfloat16),
            grad_doc,
            preferred_element_type=jnp.float32,
        )
        grad_parts.append(
            jnp.concatenate(
                [
                    grad_query.reshape(length, model_width),
                    grad_key.reshape(length, model_width),
                    grad_value.reshape(length, model_width),
                ],
                axis=1,
            )
        )
    grad_qkv = jnp.concatenate(grad_parts).astype(jnp.bfloat16)
    grad_qkv_float = grad_qkv.astype(jnp.float32)
    grad_query_bias = jnp.sum(grad_qkv_float[:, :model_width], 0)
    grad_value_bias = jnp.sum(grad_qkv_float[:, 2 * model_width :], 0)
    grad_qkv_weight = jnp.einsum(
        "rd,re->de", token_rows, grad_qkv, preferred_element_type=jnp.float32
    )
    grad_tokens = (
        jnp.einsum("re,de->rd", grad_qkv, qkv_weight, preferred_element_type=jnp.float32) + grad_one
    ).astype(jnp.bfloat16)
    matrices = (grad_qkv_weight, grad_out_weight, grad_up_weight, grad_down_weight)
    partial_sums = (
        lax.psum_scatter(
            matrices[0].astype(jnp.bfloat16), "wide", scatter_dimension=1, tiled=True
        ).astype(jnp.float32),
        lax.psum_scatter(
            matrices[1].astype(jnp.bfloat16), "wide", scatter_dimension=1, tiled=True
        ).astype(jnp.float32),
        lax.psum_scatter(
            matrices[2].astype(jnp.bfloat16), "wide", scatter_dimension=1, tiled=True
        ).astype(jnp.float32),
        lax.psum_scatter(
            matrices[3].astype(jnp.bfloat16), "wide", scatter_dimension=1, tiled=True
        ).astype(jnp.float32),
    )
    summed_mats = (
        lax.psum_scatter(
            partial_sums[0].astype(jnp.bfloat16), "narrow", scatter_dimension=0, tiled=True
        ).astype(jnp.float32),
        lax.psum_scatter(
            partial_sums[1].astype(jnp.bfloat16), "narrow", scatter_dimension=0, tiled=True
        ).astype(jnp.float32),
        lax.psum_scatter(
            partial_sums[2].astype(jnp.bfloat16), "narrow", scatter_dimension=0, tiled=True
        ).astype(jnp.float32),
        lax.psum_scatter(
            partial_sums[3].astype(jnp.bfloat16), "narrow", scatter_dimension=0, tiled=True
        ).astype(jnp.float32),
    )
    smalls = lax.psum(
        (
            grad_query_bias,
            grad_value_bias,
            grad_out_bias,
            grad_first_gain,
            grad_first_shift,
            grad_up_bias,
            grad_down_bias,
            grad_second_gain,
            grad_second_shift,
            grad_dir_weight,
            grad_dir_bias,
        ),
        ("wide", "narrow"),
    )
    return (
        encoded_rows.reshape(tokens.shape),
        grad_tokens.reshape(tokens.shape),
        summed_mats[0],
        smalls[0],
        smalls[1],
        summed_mats[1],
        smalls[2],
        smalls[3],
        smalls[4],
        summed_mats[2],
        smalls[5],
        summed_mats[3],
        smalls[6],
        smalls[7],
        smalls[8],
        smalls[9],
        smalls[10],
    )


def solution(mesh):
    placed = (
        P(("wide", "narrow"), None, None),
        P(("wide", "narrow")),
        P(),
        P(),
        P(),
        P(),
        P(),
        P(),
        P(),
        P(),
        P(),
        P(),
        P(),
        P(),
        P(),
        P(),
        P(),
        P(("wide", "narrow"), None),
        P(("wide", "narrow"), None),
        P(("wide", "narrow"), None, None),
        P(("wide", "narrow"), None),
        P(("wide", "narrow"), None, None),
    )
    return jax.shard_map(
        on_device,
        mesh=mesh,
        in_specs=placed,
        out_specs=(
            P(("wide", "narrow"), None, None),
            P(("wide", "narrow"), None, None),
            P("narrow", "wide"),
            P(),
            P(),
            P("narrow", "wide"),
            P(),
            P(),
            P(),
            P("narrow", "wide"),
            P(),
            P("narrow", "wide"),
            P(),
            P(),
            P(),
            P(),
            P(),
        ),
        check_vma=False,
    )
```

profile of v0, /device:TPU:0, one launch (start us, length us, event | category | flops | bytes accessed | tf_op | source)
XLA Modules:
  0.0 747.8 jit_solution(5606578285930874321)
XLA Ops:
  20.7 5.9 add_convert_fusion
  67.2 13.3 %multiply_convert_fusion.2 = (bf16[1024,3072]{1,0:T(8,128)(2,1)S(1)}, f32[1024,3072]{1,0:T(8,128)}) fusion(f32[3072]{0:T(1024)S(1)} %copy-done.46, bf16[768,3072]{1,0:T(8,128)(2,1)} %param.31, f32[1024,768]{1,0:T(8,128)S(1)} %get-tuple-element.114, f32[768]{0:T(1024)S(1)} %copy-done.50, f32[768]{0:T(1024)S(1)} %convert_element_type.164, ...), kind=kOutput, calls=%fused_computation.22 | convolution fusion | flops 4854644736 | bytes 26765312 | tf_op jit(solution)/shard_map/dot_general | solution.py:113
  94.5 7.5 %all-to-all-start = ((bf16[8,32,768]{2,1,0:T(8,128)(2,1)}), bf16[8,32,768]{2,1,0:T(8,128)(2,1)}, u32[]{:S(2)}, u32[]{:S(2)}) async-start(bf16[8,32,768]{2,1,0:T(8,128)(2,1)} %bitcast.144), calls=%async_computation | async-start | bytes 786432 | tf_op jit(solution)/shard_map/all_to_all | solution.py:132
  105.1 8.6 %all-to-all-done = bf16[8,32,768]{2,1,0:T(8,128)(2,1)} async-done(((bf16[8,32,768]{2,1,0:T(8,128)(2,1)}), bf16[8,32,768]{2,1,0:T(8,128)(2,1)}, u32[]{:S(2)}, u32[]{:S(2)}) %all-to-all-start) | async-done | bytes 393248 | tf_op jit(solution)/shard_map/all_to_all | solution.py:132
  154.2 8.2 %scatter_custom_fusion.3 = f32[1024,768]{1,0:T(8,128)} fusion(f32[1024,768]{1,0:T(8,128)} %bitcast_convert_fusion, s32[256]{0:T(256)} %bitcast.154, bf16[256,768]{1,0:T(8,128)(2,1)} %bitcast.24, s32[1024]{0:T(1024)} %pad_clamp_fusion), kind=kCustom, calls=%fused_computation.84 | custom fusion | flops 393216 | bytes 3543040 | tf_op jit(solution)/shard_map/scatter-add | solution.py:171
  169.7 13.4 %convert_reduce_fusion = (f32[3072]{0:T(1024)}, bf16[1024,3072]{1,0:T(8,128)(2,1)S(1)}) fusion(f32[1024,3072]{1,0:T(8,128)} %get-tuple-element.116, f32[3072]{0:T(1024)S(1)} %copy-done.47, bf16[3072,768]{1,0:T(8,128)(2,1)S(1)} %bitcast.165, f32[1024,768]{1,0:T(8,128)S(1)} %get-tuple-element.94), kind=kOutput, calls=%fused_computation.15 | convolution fusion | flops 4873516032 | bytes 26763264 | tf_op jit(solution)/shard_map/rd,fd->rf/dot_general | solution.py:182
  183.2 6.5 multiply_reduce_fusion.3
  199.7 10.6 %multiply_reduce_fusion.1 = (f32[12,512]{1,0:T(8,128)S(1)}, f32[12,512,512]{1,2,0:T(8,128)}) fusion(f32[12,512,512]{1,2,0:T(8,128)} %copy-done.1, f32[12,512]{1,0:T(8,128)S(1)} %copy-done.28, bf16[512,12,64]{0,2,1:T(8,128)(2,1)S(1)} %bitcast.114, bf16[512,12,64]{0,2,1:T(8,128)(2,1)S(1)} %bitcast.131), kind=kOutput, calls=%fused_computation.20 | convolution fusion | flops 412084224 | bytes 26787840 | tf_op jit(solution)/shard_map/qhd,khd->hqk/dot_general | solution.py:216
  212.5 10.8 %multiply_convert_fusion.1 = bf16[12,512,512]{1,2,0:T(8,128)(2,1)} fusion(f32[12,512,512]{1,2,0:T(8,128)} %get-tuple-element.125, f32[12,512,512]{1,2,0:T(8,128)S(1)} %bitcast.104, f32[12,512]{1,0:T(8,128)S(1)} %get-tuple-element.124, f32[12,512]{1,0:T(8,128)S(1)} %copy-done.28), kind=kLoop, calls=%fused_computation.19 | loop fusion | flops 12582912 | bytes 31506432 | tf_op jit(solution)/shard_map/convert_element_type | solution.py:220
  237.0 6.7 multiply_reduce_fusion
  243.7 10.7 %multiply_convert_fusion = bf16[12,512,512]{1,2,0:T(8,128)(2,1)S(1)} fusion(f32[12,512,512]{1,2,0:T(8,128)} %get-tuple-element.123, f32[12,512,512]{1,2,0:T(8,128)} %copy-done.2, f32[12,512]{1,0:T(8,128)} %get-tuple-element.122, f32[12,512]{1,0:T(8,128)} %log_add_fusion), kind=kLoop, calls=%fused_computation.16 | loop fusion | flops 12582912 | bytes 31506432 | tf_op jit(solution)/shard_map/convert_element_type | solution.py:220
  261.1 29.5 %fusion.18 = bf16[768,2304]{0,1:T(8,128)(2,1)} fusion(bf16[1024,768]{1,0:T(8,128)(2,1)S(1)} %bitcast.170, bf16[512,768]{0,1:T(8,128)(2,1)S(1)} %bitcast.134, bf16[512,768]{0,1:T(8,128)(2,1)S(1)} %bitcast.141, bf16[512,768]{0,1:T(8,128)(2,1)S(1)} %bitcast.125, bf16[512,768]{0,1:T(8,128)(2,1)S(1)} %bitcast.135, bf16[512,768]{0,1:T(8,128)(2,1)S(1)} %bitcast.140, ...), kind=kOutput, calls=%fused_computation.45 | convolution fusion | flops 3653959680 | bytes 9830400 | tf_op jit(solution)/shard_map/rd,re->de/dot_general | solution.py:249
  290.7 10.7 %convolution_convert_fusion.1 = bf16[768,3072]{1,0:T(8,128)(2,1)} fusion(bf16[1024,3072]{1,0:T(8,128)(2,1)} %copy-done.63, f32[1024,768]{1,0:T(8,128)} %copy-done.6, f32[768]{0:T(1024)} %convert_element_type.165, f32[768]{0:T(1024)S(1)} %copy-done.42, f32[1024]{0:T(1024)} %copy-done.43, f32[1024]{0:T(1024)S(1)} %copy-done.40), kind=kOutput, calls=%fused_computation.42 | convolution fusion | flops 4838129664 | bytes 14170112 | tf_op jit(solution)/shard_map/rd,rf->df/dot_general | solution.py:187
  301.4 6.7 copy.105
  308.2 10.1 %convolution_convert_fusion = bf16[3072,768]{0,1:T(8,128)(2,1)} fusion(bf16[1024,3072]{1,0:T(8,128)(2,1)} %copy-done.64, f32[1024,768]{1,0:T(8,128)} %copy-done.22), kind=kOutput, calls=%fused_computation.41 | convolution fusion | flops 4834983936 | bytes 14155776 | tf_op jit(solution)/shard_map/rf,rd->fd/dot_general | solution.py:178
  320.2 68.8 %reduce-scatter.15.cloned.1.call-done = bf16[768,288]{0,1:T(8,128)(2,1)} async-done(((bf16[768,2304]{0,1:T(8,128)(2,1)}), bf16[768,288]{0,1:T(8,128)(2,1)}) %reduce-scatter.15.cloned.1.call-update) | async-done | bytes 442384 | tf_op jit(solution)/shard_map/reduce_scatter | solution.py:257
  391.1 96.3 %reduce-scatter.29.cloned.1.call-done = bf16[384,768]{1,0:T(8,128)(2,1)} async-done(((bf16[3072,768]{1,0:T(8,128)(2,1)}), bf16[384,768]{1,0:T(8,128)(2,1)}) %reduce-scatter.29.cloned.1.call-update) | async-done | bytes 589840
  493.4 92.6 %reduce-scatter.21.cloned.1.call-done = bf16[3072,96]{0,1:T(8,128)(2,1)} async-done(((bf16[3072,768]{0,1:T(8,128)(2,1)}), bf16[3072,96]{0,1:T(8,128)(2,1)}) %reduce-scatter.21.cloned.1.call-update) | async-done | bytes 589840 | tf_op jit(solution)/shard_map/reduce_scatter | solution.py:266
  587.7 7.3 fusion.54
  598.9 8.4 %add_convert_fusion.1 = bf16[1024,768]{1,0:T(8,128)(2,1)} fusion(f32[1024,768]{1,0:T(8,128)} %copy-done.25, bf16[768,2304]{1,0:T(8,128)(2,1)S(1)} %copy-done, bf16[512,768]{0,1:T(8,128)(2,1)} %bitcast.133, bf16[512,768]{0,1:T(8,128)(2,1)} %bitcast.143, bf16[512,768]{0,1:T(8,128)(2,1)} %bitcast.127, bf16[512,768]{0,1:T(8,128)(2,1)} %bitcast.137, ...), kind=kOutput, calls=%fused_computation.52 | convolution fusion | flops 3653763072 | bytes 12976128 | tf_op jit(solution)/shard_map/re,de->rd/dot_general | solution.py:253
  611.5 21.5 %reduce-scatter.25.cloned.1.call-done = bf16[192,288]{1,0:T(8,128)(2,1)} async-done(((bf16[768,288]{1,0:T(8,128)(2,1)}), bf16[192,288]{1,0:T(8,128)(2,1)}) %reduce-scatter.25.cloned.1.call-update) | async-done | bytes 110608
  636.5 21.3 %reduce-scatter.19.cloned.1.call-done = bf16[192,384]{1,0:T(8,128)(2,1)} async-done(((bf16[768,384]{1,0:T(8,128)(2,1)}), bf16[192,384]{1,0:T(8,128)(2,1)}) %reduce-scatter.19.cloned.1.call-update) | async-done | bytes 147472 | tf_op jit(solution)/shard_map/reduce_scatter | solution.py:277
  659.4 23.2 %reduce-scatter.23.cloned.1.call-done = bf16[768,96]{0,1:T(8,128)(2,1)} async-done(((bf16[3072,96]{0,1:T(8,128)(2,1)}), bf16[768,96]{0,1:T(8,128)(2,1)}) %reduce-scatter.23.cloned.1.call-update) | async-done | bytes 147472 | tf_op jit(solution)/shard_map/reduce_scatter | solution.py:280
  684.2 41.7 %all-reduce.3.cloned.1.call-done = (f32[768]{0:T(1024)}, f32[768]{0:T(1024)}, f32[768]{0:T(1024)}, f32[768]{0:T(1024)}, f32[768]{0:T(1024)}, /*index=5*/f32[3072...) async-done(((f32[768]{0:T(1024)}, f32[768]{0:T(1024)}, f32[768]{0:T(1024)}, f32[768]{0:T(1024)}, f32[768]{0:T(1024)}, ...) | async-done | bytes 86064 | tf_op jit(solution)/shard_map/psum | solution.py:284
  (286 shorter events, 190.4 us)
Async XLA Ops:
  11.0 69.6 %copy-start.41 = (f32[768]{0:T(1024)}, f32[768]{0:T(1024)S(1)}, u32[]{:S(2)}) copy-start(f32[768]{0:T(1024)S(1)} %convert_element_type.164) | copy-start | bytes 9220
  18.1 68.6 %copy-start.35 = (f32[1,4,2,128]{3,1,2,0:T(4,128)}, f32[1,4,2,128]{3,1,2,0:T(4,128)S(1)}, u32[]{:S(2)}) copy-start(f32[1,4,2,128]{3,1,2,0:T(4,128)S(1)} %copy.107) | copy-start | bytes 12292
  28.8 13.9 %copy-start.55 = (pred[512]{0:T(512)(128)(4,1)S(1)}, pred[512]{0:T(512)(128)(4,1)}, u32[]{:S(2)}) copy-start(pred[512]{0:T(512)(128)(4,1)} %get-tuple-element.78) | copy-start | bytes 1540
  66.6 14.0 %copy-start.6 = (f32[1024,768]{1,0:T(8,128)}, f32[1024,768]{1,0:T(8,128)S(1)}, u32[]{:S(2)}) copy-start(f32[1024,768]{1,0:T(8,128)S(1)} %get-tuple-element.114) | copy-start | bytes 9437188
  66.6 14.0 %copy-start.39 = (f32[1024]{0:T(1024)}, f32[1024]{0:T(1024)S(1)}, u32[]{:S(2)}) copy-start(f32[1024]{0:T(1024)S(1)} %broadcast_multiply_fusion.5) | copy-start | bytes 12292
  66.6 14.0 %slice-start.9 = ((s8[4718592]{0:T(1024)(128)(4,1)}), s8[4194304]{0:T(1024)(128)(4,1)S(1)}, s32[]{:S(2)}) async-start(s8[4718592]{0:T(1024)(128)(4,1)} %bitcast.162), calls=%async_computation.28 | async-start | bytes 8388608
  86.7 30.4 %copy-start.37 = (f32[1024]{0:T(1024)}, f32[1024]{0:T(1024)S(1)}, u32[]{:S(2)}) copy-start(f32[1024]{0:T(1024)S(1)} %add_rsqrt_fusion) | copy-start | bytes 12292
  94.5 19.2 %all-to-all-start = ((bf16[8,32,768]{2,1,0:T(8,128)(2,1)}), bf16[8,32,768]{2,1,0:T(8,128)(2,1)}, u32[]{:S(2)}, u32[]{:S(2)}) async-start(bf16[8,32,768]{2,1,0:T(8,128)(2,1)} %bitcast.144), calls=%async_computation | async-start | bytes 786432 | tf_op jit(solution)/shard_map/all_to_all | solution.py:132
  138.8 15.3 %all-to-all-start.1 = ((bf16[8,32,768]{2,1,0:T(8,128)(2,1)}), bf16[8,32,768]{2,1,0:T(8,128)(2,1)}, u32[]{:S(2)}, u32[]{:S(2)}) async-start(bf16[8,32,768]{2,1,0:T(8,128)(2,1)} %bitcast.145), calls=%async_computation.1 | async-start | bytes 786432 | tf_op jit(solution)/shard_map/all_to_all | solution.py:166
  142.9 175.4 %reduce-scatter.17.cloned.1.call-start = ((), (), s32[]{:S(2)}) async-start(), calls=%async_computation.11 | async-start | bytes 1327104 | tf_op jit(solution)/shard_map/reduce_scatter | solution.py:260
  167.7 15.4 %slice-start.13 = ((s8[4718592]{0:T(1024)(128)(4,1)}), s8[4194304]{0:T(1024)(128)(4,1)S(1)}, s32[]{:S(2)}) async-start(s8[4718592]{0:T(1024)(128)(4,1)} %bitcast.166), calls=%async_computation.32 | async-start | bytes 8388608
  169.6 13.5 %copy-start.22 = (f32[1024,768]{1,0:T(8,128)}, f32[1024,768]{1,0:T(8,128)S(1)}, u32[]{:S(2)}) copy-start(f32[1024,768]{1,0:T(8,128)S(1)} %get-tuple-element.94) | copy-start | bytes 9437188
  212.5 21.5 %slice-start.6 = ((s8[12582912]{0:T(1024)(128)(4,1)}), s8[4194304]{0:T(1024)(128)(4,1)S(1)}, s32[]{:S(2)}) async-start(s8[12582912]{0:T(1024)(128)(4,1)} %bitcast.107), calls=%async_computation.25 | async-start | bytes 8388608
  212.5 21.5 %slice-start.7 = ((s8[12582912]{0:T(1024)(128)(4,1)}), s8[4194304]{0:T(1024)(128)(4,1)S(1)}, s32[]{:S(2)}) async-start(s8[12582912]{0:T(1024)(128)(4,1)} %bitcast.107), calls=%async_computation.26 | async-start | bytes 8388608
  243.6 145.3 %reduce-scatter.15.cloned.1.call-start = ((), (), s32[]{:S(2)}) async-start(), calls=%async_computation.10 | async-start | bytes 3981312 | tf_op jit(solution)/shard_map/reduce_scatter | solution.py:257
  243.7 14.0 %slice-start.3 = ((s8[12582912]{0:T(1024)(128)(4,1)}), s8[4194304]{0:T(1024)(128)(4,1)S(1)}, s32[]{:S(2)}) async-start(s8[12582912]{0:T(1024)(128)(4,1)} %bitcast.105), calls=%async_computation.22 | async-start | bytes 8388608
  243.7 14.0 %slice-start.4 = ((s8[12582912]{0:T(1024)(128)(4,1)}), s8[4194304]{0:T(1024)(128)(4,1)S(1)}, s32[]{:S(2)}) async-start(s8[12582912]{0:T(1024)(128)(4,1)} %bitcast.105), calls=%async_computation.23 | async-start | bytes 8388608
  290.6 196.8 %reduce-scatter.29.cloned.1.call-start = ((), (), s32[]{:S(2)}) async-start(), calls=%async_computation.17 | async-start | bytes 5308416
  308.1 277.9 %reduce-scatter.21.cloned.1.call-start = ((), (), s32[]{:S(2)}) async-start(), calls=%async_computation.13 | async-start | bytes 5308416 | tf_op jit(solution)/shard_map/reduce_scatter | solution.py:266
  318.3 290.2 %reduce-scatter.27.cloned.1.call-start = ((), (), s32[]{:S(2)}) async-start(), calls=%async_computation.16 | async-start | bytes 245760
  320.1 312.9 %reduce-scatter.25.cloned.1.call-start = ((), (), s32[]{:S(2)}) async-start(), calls=%async_computation.15 | async-start | bytes 737280
  391.0 266.8 %reduce-scatter.19.cloned.1.call-start = ((), (), s32[]{:S(2)}) async-start(), calls=%async_computation.12 | async-start | bytes 737280 | tf_op jit(solution)/shard_map/reduce_scatter | solution.py:277
  489.6 193.0 %reduce-scatter.23.cloned.1.call-start = ((), (), s32[]{:S(2)}) async-start(), calls=%async_computation.14 | async-start | bytes 737280 | tf_op jit(solution)/shard_map/reduce_scatter | solution.py:280
  586.0 139.9 %all-reduce.3.cloned.1.call-start = ((), (), s32[]{:S(2)}) async-start(), calls=%async_computation.18 | async-start | bytes 189440 | tf_op jit(solution)/shard_map/psum | solution.py:284
  (67 other events, 389.8 us)
Sparse Core Ops, SparseCore 0:
  243.8 63.2 reduce-scatter.16
  310.7 78.1 reduce-scatter.14
  392.6 94.7 reduce-scatter.28
  490.9 95.0 reduce-scatter.20
  588.9 19.5 reduce-scatter.26
  610.8 22.1 reduce-scatter.24
  635.7 22.0 reduce-scatter.18
  660.4 22.1 reduce-scatter.22
Sparse Core Ops, SparseCore 1:
  599.0 126.9 all-reduce.2
where the time goes:
time: 756 us; the launch traced here: 748 us
  waiting for transfers between devices  379 us (50%)
  matrix products  170 us (22%)
  other arithmetic  94.7 us (13%)
  local copies, waits for them, and re-layouts  74.2 us (10%)
  between operations  17.1 us (2%)
  starting transfers between devices  12.3 us (2%)
    unnamed x12, waiting for transfers between devices  119 us
    reduce_scatter x1, waiting for transfers between devices, on_device(): lax.psum_scatter(matrices[3].astype(jnp.bfloat16), 'wide', scatter_dimens...  92.6 us
    reduce_scatter x1, waiting for transfers between devices, on_device(): lax.psum_scatter(matrices[0].astype(jnp.bfloat16), 'wide', scatter_dimens...  68.8 us
    unnamed x180, local copies, waits for them, and re-layouts  46 us
    psum x1, waiting for transfers between devices, on_device(): lax.psum((grad_query_bias, grad_value_bias, grad_out_bias, grad_first_gai...  41.7 us
    dot_general x1, matrix products, on_device(): jnp.einsum('rd,re->de', token_rows, grad_qkv, preferred_element_type=jnp....  29.5 us
    reduce_scatter x1, waiting for transfers between devices, on_device(): lax.psum_scatter(partial_sums[3].astype(jnp.bfloat16), 'narrow', scatter_...  23.2 us
    convert_element_type x2, other arithmetic, on_device(): grad_scores = (attention * (grad_chance - inner)).astype(jnp.bfloat16)  21.5 us
  transfers between devices with their start and end apart: 11, of which 10 were waited for; matrix products, arithmetic and copies ran while one was open for 16% of the time, Pallas kernels for 0%

commit v1 on v0

--- a/solution.py
+++ b/solution.py
@@ -1,6 +1,8 @@
 import jax
 import jax.numpy as jnp
 from jax import lax
+from jax.experimental import pallas as pl
+from jax.experimental.pallas import tpu as pltpu
 from jax.sharding import PartitionSpec as P
 
 HEADS = 12
@@ -33,6 +35,492 @@
 
 def normal_cdf(values):
     return 0.5 * (1.0 + lax.erf(values * 0.7071067811865476))
+
+
+MESH_ID = pl.DeviceIdType.MESH
+
+
+def axis_bits():
+    names = []
+    for axis in ("wide", "narrow"):
+        count = lax.axis_size(axis).bit_length() - 1
+        names += [(axis, bit) for bit in reversed(range(count))]
+    return names
+
+
+class Place:
+    def __init__(self):
+        self.index = {axis: lax.axis_index(axis) for axis in ("wide", "narrow")}
+        self.names = axis_bits()
+        self.bit = {name: (self.index[name[0]] // (1 << name[1])) % 2 for name in self.names}
+
+    def across(self, name):
+        axis, bit = name
+        target = dict(self.index)
+        target[axis] = target[axis] + (1 << bit) - (2 << bit) * self.bit[name]
+        return target
+
+    def greet(self):
+        barrier = pltpu.get_barrier_semaphore()
+        for name in self.names:
+            pl.semaphore_signal(barrier, inc=1, device_id=self.across(name), device_id_type=MESH_ID)
+        pl.semaphore_wait(barrier, len(self.names))
+
+
+class Halving:
+    def __init__(self, place, order, source, own, received, send_sems, recv_sems, first_sem):
+        self.place, self.order = place, order
+        self.source, self.own, self.received = source, own, received
+        self.send_sems, self.recv_sems, self.first_sem = send_sems, recv_sems, first_sem
+        self.copies = {}
+
+    def region(self, step, mine):
+        index = []
+        for name in self.place.names:
+            if name in self.order[:step]:
+                index.append(self.place.bit[name])
+            elif name == self.order[step]:
+                index.append(self.place.bit[name] if mine else 1 - self.place.bit[name])
+            else:
+                index.append(slice(None))
+        return tuple(index)
+
+    def send(self, step):
+        held = self.source if step == 0 else self.own
+        self.copies[step] = pltpu.make_async_remote_copy(
+            src_ref=held.at[self.region(step, False)],
+            dst_ref=self.received[step],
+            send_sem=self.send_sems.at[self.first_sem + step],
+            recv_sem=self.recv_sems.at[self.first_sem + step],
+            device_id=self.place.across(self.order[step]),
+            device_id_type=MESH_ID,
+        )
+        self.copies[step].start()
+
+    def add(self, step):
+        self.copies[step].wait_recv()
+        mine = self.region(step, True)
+        if step + 1 < len(self.order):
+            self.own[mine] = self.own[mine] + self.received[step][...]
+            return None
+        return self.own[mine].astype(jnp.float32) + self.received[step][...].astype(jnp.float32)
+
+    def close(self):
+        for copy in self.copies.values():
+            copy.wait_send()
+
+
+def received_shapes(names, order, block):
+    left = len(names)
+    shapes = []
+    for _ in order:
+        left -= 1
+        shapes.append((2,) * left + block)
+    return shapes
+
+
+def link_orders():
+    wide = [("wide", bit) for bit in range(lax.axis_size("wide").bit_length() - 1)]
+    narrow = [("narrow", bit) for bit in range(1, lax.axis_size("narrow").bit_length() - 1)]
+    core = [("narrow", 0)]
+    return {
+        "y_x_z": core + narrow + wide,
+        "x_y_z": core + wide[:1] + narrow + wide[1:],
+        "x_z_y": core + wide + narrow,
+        "y_z_x": core + narrow + wide[1:] + wide[:1],
+    }
+
+
+def reduce_all(*operands):
+    arrays, flat = operands[:-1], operands[-1]
+    names = axis_bits()
+    steps = len(names)
+    orders = link_orders()
+    pieces = [(0, orders["y_x_z"]), (1, orders["x_y_z"]), (2, orders["x_z_y"]), (3, orders["y_z_x"])]
+    count = len(pieces)
+    blocks = [array.shape[-2:] for array in arrays]
+
+    def kernel(*refs):
+        sources, small = refs[:count], refs[count]
+        outs, small_out = refs[count + 1 : 2 * count + 1], refs[2 * count + 1]
+        rest = list(refs[2 * count + 2 :])
+        owns = [rest.pop(0) for _ in range(count)]
+        received = [[rest.pop(0) for _ in range(steps)] for _ in range(count)]
+        small_sent, small_received = rest.pop(0), rest.pop(0)
+        send_sems, recv_sems, local_sems = rest
+        place = Place()
+        place.greet()
+        running = []
+        local = []
+        for number, (array, order) in enumerate(pieces):
+            item = Halving(
+                place, order, sources[array], owns[array], received[array], send_sems, recv_sems, number * steps
+            )
+            item.send(0)
+            keep = item.region(0, True)
+            copy = pltpu.make_async_copy(
+                sources[array].at[keep], owns[array].at[keep], local_sems.at[number]
+            )
+            copy.start()
+            running.append(item)
+            local.append(copy)
+        small_sent[0] = small[...]
+        small_copies = []
+        last_sem = count * steps
+        for step in range(steps):
+            copy = pltpu.make_async_remote_copy(
+                src_ref=small_sent.at[step],
+                dst_ref=small_received.at[step],
+                send_sem=send_sems.at[last_sem + step],
+                recv_sem=recv_sems.at[last_sem + step],
+                device_id=place.across(orders["x_y_z"][step]),
+                device_id_type=MESH_ID,
+            )
+            copy.start()
+            small_copies.append(copy)
+            for number, item in enumerate(running):
+                if step == 0:
+                    local[number].wait()
+                total = item.add(step)
+                if total is None:
+                    item.send(step + 1)
+                elif number < 2:
+                    outs[number][...] = total
+                else:
+                    outs[number][place.bit["narrow", 0]] = total
+            copy.wait_recv()
+            if step + 1 < steps:
+                small_sent[step + 1] = small_sent[step] + small_received[step]
+            else:
+                small_out[...] = small_sent[step] + small_received[step]
+        swaps = []
+        for slot, number in enumerate((2, 3)):
+            mine = outs[number].at[place.bit["narrow", 0]]
+            copy = pltpu.make_async_remote_copy(
+                src_ref=mine,
+                dst_ref=mine,
+                send_sem=send_sems.at[last_sem + steps + slot],
+                recv_sem=recv_sems.at[last_sem + steps + slot],
+                device_id=place.across(("narrow", 0)),
+                device_id_type=MESH_ID,
+            )
+            copy.start()
+            swaps.append(copy)
+        for copy in swaps:
+            copy.wait()
+        for item in running:
+            item.close()
+        for copy in small_copies:
+            copy.wait_send()
+
+    scratch = [pltpu.VMEM(array.shape, jnp.bfloat16) for array in arrays]
+    for number, (array, order) in enumerate(pieces):
+        scratch += [pltpu.VMEM(shape, jnp.bfloat16) for shape in received_shapes(names, order, blocks[array])]
+    scratch += [pltpu.VMEM((steps,) + flat.shape, jnp.float32)] * 2
+    sems = count * steps + steps + 2
+    scratch += [pltpu.SemaphoreType.DMA((sems,)), pltpu.SemaphoreType.DMA((sems,)), pltpu.SemaphoreType.DMA((count,))]
+    out_shape = [jax.ShapeDtypeStruct(blocks[0], jnp.float32), jax.ShapeDtypeStruct(blocks[1], jnp.float32)]
+    out_shape += [jax.ShapeDtypeStruct((2,) + blocks[number], jnp.float32) for number in (2, 3)]
+    out_shape += [jax.ShapeDtypeStruct(flat.shape, jnp.float32)]
+    return pl.pallas_call(
+        kernel,
+        out_shape=out_shape,
+        in_specs=[pl.BlockSpec(memory_space=pl.ANY)] * count + [pl.BlockSpec(memory_space=pltpu.VMEM)],
+        out_specs=[pl.BlockSpec(memory_space=pltpu.VMEM)] * (count + 1),
+        scratch_shapes=scratch,
+        compiler_params=pltpu.CompilerParams(
+            collective_id=0, has_side_effects=True, vmem_limit_bytes=60 << 20
+        ),
+        name="reduce_all",
+    )(*operands)
+
+
+def on_device_fast(
+    tokens,
+    doc_lengths,
+    qkv_weight,
+    query_bias,
+    value_bias,
+    out_weight,
+    out_bias,
+    first_gain,
+    first_shift,
+    up_weight,
+    up_bias,
+    down_weight,
+    down_bias,
+    second_gain,
+    second_shift,
+    dir_weight,
+    dir_bias,
+    segment_rows,
+    segment_slots,
+    pair_rows,
+    pair_labels,
+    out_cotangent,
+):
+    doc_count, length, model_width = tokens.shape
+    score_scale = HEAD_DIM ** (-0.5)
+    token_rows = tokens.reshape(doc_count * length, model_width)
+    allowed = lax.broadcasted_iota(jnp.int32, (doc_count, length), 1) < doc_lengths[:, None]
+    allowed_rows = allowed.reshape(-1, 1).astype(jnp.float32)
+    bias_row = jnp.concatenate([query_bias, jnp.zeros_like(query_bias), value_bias]).astype(
+        jnp.float32
+    )
+    qkv = (jnp.dot(token_rows, qkv_weight, preferred_element_type=jnp.float32) + bias_row).astype(
+        jnp.bfloat16
+    )
+
+    def split_heads(doc_block, which):
+        return doc_block[:, which * model_width : (which + 1) * model_width].reshape(
+            length, HEADS, HEAD_DIM
+        )
+
+    def scores_of(queries, key_rows, doc_mask):
+        scores = (
+            jnp.einsum("qhd,khd->hqk", queries, key_rows, preferred_element_type=jnp.float32)
+            * score_scale
+        )
+        return jnp.where(doc_mask[None, None, :], scores, MASKED)
+
+    mixed_parts = []
+    log_totals = []
+    for doc_index in range(doc_count):
+        doc_block = qkv[doc_index * length : (doc_index + 1) * length]
+        queries = split_heads(doc_block, 0)
+        key_rows = split_heads(doc_block, 1)
+        value_rows = split_heads(doc_block, 2)
+        scores = scores_of(queries, key_rows, allowed[doc_index])
+        highest = jnp.max(scores, -1, keepdims=True)
+        powers = jnp.exp(scores - highest)
+        summed = jnp.sum(powers, -1, keepdims=True)
+        attention = (powers / summed).astype(jnp.bfloat16)
+        log_totals.append(highest + jnp.log(summed))
+        mixed_parts.append(
+            jnp.einsum(
+                "hqk,khd->qhd", attention, value_rows, preferred_element_type=jnp.float32
+            ).reshape(length, model_width)
+        )
+    mixed = jnp.concatenate(mixed_parts).astype(jnp.bfloat16)
+    attended = jnp.dot(mixed, out_weight, preferred_element_type=jnp.float32) + out_bias.astype(
+        jnp.float32
+    )
+    resid_one = token_rows.astype(jnp.float32) + attended
+    hidden_one, normed_one, inverse_one = norm_forward(
+        resid_one, first_gain.astype(jnp.float32), first_shift.astype(jnp.float32)
+    )
+    hidden_low = hidden_one.astype(jnp.bfloat16)
+    upper_pre = jnp.dot(hidden_low, up_weight, preferred_element_type=jnp.float32) + up_bias.astype(
+        jnp.float32
+    )
+    cumulative = normal_cdf(upper_pre)
+    active = (upper_pre * cumulative).astype(jnp.bfloat16)
+    lowered = jnp.dot(active, down_weight, preferred_element_type=jnp.float32) + down_bias.astype(
+        jnp.float32
+    )
+    resid_two = hidden_one + lowered
+    second_float = second_gain.astype(jnp.float32)
+    normed_out, normed_two, inverse_two = norm_forward(
+        resid_two, second_float, second_shift.astype(jnp.float32)
+    )
+    encoded_rows = (normed_out * allowed_rows).astype(jnp.bfloat16)
+    doc_starts = lax.broadcasted_iota(jnp.int32, (doc_count, 1), 0) * length
+    picked_rows = (segment_rows + doc_starts).reshape(-1)
+    picked = encoded_rows[picked_rows]
+    slots = segment_slots.reshape(-1)
+    outgoing = jnp.zeros_like(picked).at[slots].set(picked)
+    arrived = lax.all_to_all(outgoing, "wide", split_axis=0, concat_axis=0, tiled=True)
+    pairs = pair_rows.reshape(-1, 2)
+    labels = pair_labels.reshape(-1)
+    first_rows = arrived[pairs[:, 0]]
+    second_rows = arrived[pairs[:, 1]]
+    logits = (
+        jnp.dot(first_rows, dir_weight[:model_width], preferred_element_type=jnp.float32)
+        + jnp.dot(second_rows, dir_weight[model_width:], preferred_element_type=jnp.float32)
+        + dir_bias.astype(jnp.float32)
+    )
+    powers_head = jnp.exp(logits - jnp.max(logits, -1, keepdims=True))
+    chance = powers_head / jnp.sum(powers_head, -1, keepdims=True)
+    classes = lax.broadcasted_iota(jnp.int32, logits.shape, 1)
+    delta = chance - (labels[:, None] == classes).astype(jnp.float32)
+    first_float = first_rows.astype(jnp.float32)
+    second_rows_float = second_rows.astype(jnp.float32)
+    grad_dir_weight = jnp.concatenate(
+        [
+            jnp.dot(first_float.T, delta, precision=EXACT, preferred_element_type=jnp.float32),
+            jnp.dot(
+                second_rows_float.T, delta, precision=EXACT, preferred_element_type=jnp.float32
+            ),
+        ]
+    )
+    grad_dir_bias = jnp.sum(delta, 0)
+    dir_float = dir_weight.astype(jnp.float32)
+    grad_first = jnp.dot(
+        delta, dir_float[:model_width].T, precision=EXACT, preferred_element_type=jnp.float32
+    )
+    grad_second = jnp.dot(
+        delta, dir_float[model_width:].T, precision=EXACT, preferred_element_type=jnp.float32
+    )
+    grad_arrived = jnp.zeros((arrived.shape[0], model_width), jnp.float32)
+    grad_arrived = grad_arrived.at[pairs[:, 0]].add(grad_first).at[pairs[:, 1]].add(grad_second)
+    returned = lax.all_to_all(
+        grad_arrived.astype(jnp.bfloat16), "wide", split_axis=0, concat_axis=0, tiled=True
+    )
+    grad_picked = returned[slots].astype(jnp.float32)
+    grad_encoded = (
+        out_cotangent.reshape(-1, model_width).astype(jnp.float32).at[picked_rows].add(grad_picked)
+    )
+    grad_encoded = grad_encoded * allowed_rows
+    grad_two, grad_second_gain, grad_second_shift = norm_backward(
+        grad_encoded, normed_two, inverse_two, second_float
+    )
+    grad_lowered = grad_two.astype(jnp.bfloat16)
+    grad_down_weight = jnp.einsum(
+        "rd,rf->df", grad_lowered, active, preferred_element_type=jnp.float32
+    )
+    grad_down_bias = jnp.sum(grad_lowered.astype(jnp.float32), 0)
+    grad_active = jnp.einsum(
+        "rd,fd->rf", grad_lowered, down_weight, preferred_element_type=jnp.float32
+    )
+    density = jnp.exp(-0.5 * upper_pre * upper_pre) * 0.3989422804014327
+    grad_upper = (grad_active * (cumulative + upper_pre * density)).astype(jnp.bfloat16)
+    grad_up_weight = jnp.einsum(
+        "rd,rf->df", hidden_low, grad_upper, preferred_element_type=jnp.float32
+    )
+    grad_up_bias = jnp.sum(grad_upper.astype(jnp.float32), 0)
+    grad_hidden = grad_two + jnp.einsum(
+        "rf,df->rd", grad_upper, up_weight, preferred_element_type=jnp.float32
+    )
+    grad_one, grad_first_gain, grad_first_shift = norm_backward(
+        grad_hidden, normed_one, inverse_one, first_gain.astype(jnp.float32)
+    )
+    grad_attended = grad_one.astype(jnp.bfloat16)
+    grad_out_weight = jnp.einsum(
+        "re,rd->ed", grad_attended, mixed, preferred_element_type=jnp.float32
+    )
+    grad_out_bias = jnp.sum(grad_attended.astype(jnp.float32), 0)
+    grad_mixed = jnp.einsum(
+        "re,de->rd", grad_attended, out_weight, preferred_element_type=jnp.float32
+    ).astype(jnp.bfloat16)
+    grad_parts = []
+    for doc_index in range(doc_count):
+        doc_block = qkv[doc_index * length : (doc_index + 1) * length]
+        queries = split_heads(doc_block, 0)
+        key_rows = split_heads(doc_block, 1)
+        value_rows = split_heads(doc_block, 2)
+        scores = scores_of(queries, key_rows, allowed[doc_index])
+        attention = jnp.exp(scores - log_totals[doc_index])
+        grad_doc = grad_mixed[doc_index * length : (doc_index + 1) * length].reshape(
+            length, HEADS, HEAD_DIM
+        )
+        grad_chance = jnp.einsum(
+            "qhd,khd->hqk", grad_doc, value_rows, preferred_element_type=jnp.float32
+        )
+        inner = jnp.sum(grad_chance * attention, -1, keepdims=True)
+        grad_scores = (attention * (grad_chance - inner)).astype(jnp.bfloat16)
+        grad_query = (
+            jnp.einsum("hqk,khd->qhd", grad_scores, key_rows, preferred_element_type=jnp.float32)
+            * score_scale
+        )
+        grad_key = (
+            jnp.einsum("hqk,qhd->khd", grad_scores, queries, preferred_element_type=jnp.float32)
+            * score_scale
+        )
+        grad_value = jnp.einsum(
+            "hqk,qhd->khd",
+            attention.astype(jnp.bfloat16),
+            grad_doc,
+            preferred_element_type=jnp.float32,
+        )
+        grad_parts.append(
+            jnp.concatenate(
+                [
+                    grad_query.reshape(length, model_width),
+                    grad_key.reshape(length, model_width),
+                    grad_value.reshape(length, model_width),
+                ],
+                axis=1,
+            )
+        )
+    grad_qkv = jnp.concatenate(grad_parts).astype(jnp.bfloat16)
+    grad_qkv_float = grad_qkv.astype(jnp.float32)
+    grad_query_bias = jnp.sum(grad_qkv_float[:, :model_width], 0)
+    grad_value_bias = jnp.sum(grad_qkv_float[:, 2 * model_width :], 0)
+    grad_qkv_weight = jnp.einsum(
+        "re,rd->ed", grad_qkv, token_rows, preferred_element_type=jnp.float32
+    )
+    grad_tokens = (
+        jnp.einsum("re,de->rd", grad_qkv, qkv_weight, preferred_element_type=jnp.float32) + grad_one
+    ).astype(jnp.bfloat16)
+    wide, narrow = lax.axis_size("wide"), lax.axis_size("narrow")
+    ff = up_weight.shape[1]
+    bits = (2,) * (wide.bit_length() - 1 + narrow.bit_length() - 1)
+    half = narrow // 2
+
+    def low(values):
+        return values.astype(jnp.bfloat16)
+
+    blocks_down = low(grad_down_weight).reshape(wide, model_width // wide, narrow, ff // narrow)
+    blocks_down = blocks_down.transpose(0, 2, 1, 3).reshape(bits + (model_width // wide, ff // narrow))
+    blocks_up = low(grad_up_weight).reshape(narrow, model_width // narrow, wide, ff // wide)
+    blocks_up = blocks_up.transpose(2, 0, 1, 3).reshape(bits + (model_width // narrow, ff // wide))
+
+    def by_row_half(matrix):
+        rows = matrix.shape[0] // wide // 2
+        blocks = low(matrix).reshape(wide, 2, rows, half, model_width // half)
+        return blocks.transpose(0, 3, 1, 2, 4).reshape(bits + (rows, model_width // half))
+
+    smalls_in = (
+        grad_query_bias,
+        grad_value_bias,
+        grad_out_bias,
+        grad_first_gain,
+        grad_first_shift,
+        grad_up_bias,
+        grad_down_bias,
+        grad_second_gain,
+        grad_second_shift,
+        grad_dir_weight,
+        grad_dir_bias,
+    )
+    sizes = [item.size for item in smalls_in]
+    flat = jnp.concatenate([item.reshape(-1) for item in smalls_in])
+    flat = jnp.pad(flat, (0, -flat.size % 1024)).reshape(-1, 128)
+    out_down, out_up, out_qkv, out_out, flat = reduce_all(
+        blocks_down, blocks_up, by_row_half(grad_qkv_weight), by_row_half(grad_out_weight), flat
+    )
+    flat = flat.reshape(-1)
+    smalls = []
+    start = 0
+    for item, size in zip(smalls_in, sizes):
+        smalls.append(flat[start : start + size].reshape(item.shape))
+        start += size
+    core = lax.axis_index("narrow") % 2
+    width = model_width // narrow
+
+    def own_lanes(halves):
+        rows = halves.reshape(-1, halves.shape[-1])
+        return lax.dynamic_slice_in_dim(rows, core * width, width, 1).T
+
+    return (
+        encoded_rows.reshape(tokens.shape),
+        grad_tokens.reshape(tokens.shape),
+        own_lanes(out_qkv),
+        smalls[0],
+        smalls[1],
+        own_lanes(out_out),
+        smalls[2],
+        smalls[3],
+        smalls[4],
+        out_up,
+        smalls[5],
+        out_down.T,
+        smalls[6],
+        smalls[7],
+        smalls[8],
+        smalls[9],
+        smalls[10],
+    )
 
 
 def on_device(
@@ -318,6 +806,16 @@
     )
 
 
+def fits_blocks(mesh):
+    wide, narrow = mesh.shape["wide"], mesh.shape["narrow"]
+    width, ff = HEADS * HEAD_DIM, 4 * HEADS * HEAD_DIM
+    if narrow % 2 or wide & (wide - 1) or narrow & (narrow - 1):
+        return False
+    lanes = (ff // narrow, ff // wide, 2 * width // narrow)
+    rows = (width // wide, width // narrow, width // wide // 2, 3 * width // wide // 2)
+    return all(size % 128 == 0 for size in lanes) and all(size % 16 == 0 for size in rows)
+
+
 def solution(mesh):
     placed = (
         P(("wide", "narrow"), None, None),
@@ -344,7 +842,7 @@
         P(("wide", "narrow"), None, None),
     )
     return jax.shard_map(
-        on_device,
+        on_device_fast if fits_blocks(mesh) else on_device,
         mesh=mesh,
         in_specs=placed,
         out_specs=(

time: 756 us -> 511 us (0.68)
  waiting for transfers between devices: 379 us -> 4.59 us
  Pallas kernels: 0 us -> 109 us
  local copies, waits for them, and re-layouts: 74.2 us -> 105 us
  between operations: 17.1 us -> 1.97 us
    reduce_scatter x5 -> x0, waiting for transfers between devices: 206 us -> none  [the longest x1 92.6 us: on_device(): lax.psum_scatter(matrices[3].astype(jnp.bfloat16), 'wide', scatter_dimens...]
    unnamed x12 -> x0, waiting for transfers between devices: 119 us -> none
    pallas_call x0 -> x1, Pallas kernels: none -> 109 us  [reduce_all(): pl.pallas_call(kernel, out_shape=out_shape, in_specs=[pl.BlockSpec(memory...]
    psum x1 -> x0, waiting for transfers between devices: 41.7 us -> none  [on_device(): lax.psum((grad_query_bias, grad_value_bias, grad_out_bias, grad_first_gai...]
    reshape x0 -> x10, local copies, waits for them, and re-layouts: none -> 41.4 us  [the longest x4 18.4 us: by_row_half(): blocks = low(matrix).reshape(wide, 2, rows, half, model_width // half)]
    unnamed x180 -> x183, local copies, waits for them, and re-layouts: 46 us -> 24.4 us
    all_to_all x2, waiting for transfers between devices: 12.5 us -> 4.59 us  [the longest x1 3.98 us: on_device_fast(): lax.all_to_all(grad_arrived.astype(jnp.bfloat16), 'wide', split_axis=0, c...]
    convert_element_type x17 -> x15, other arithmetic: 48.6 us -> 53.3 us  [the longest x1 19.2 us: on_device_fast(): grad_qkv_float = grad_qkv.astype(jnp.float32)]
  transfers between devices with their start and end apart: 11 -> 2, of which waited for: 10 -> 2; matrix products, arithmetic and copies ran while one was open for 16% -> 4% of each run, Pallas kernels for 0% -> 0%
where the time goes in v1:
time: 511 us; the launch traced here: 501 us
  matrix products  170 us (33%)
  Pallas kernels  109 us (21%)
  local copies, waits for them, and re-layouts  105 us (21%)
  other arithmetic  98 us (19%)
  starting transfers between devices  12.9 us (3%)
    pallas_call x1, Pallas kernels, reduce_all(): pl.pallas_call(kernel, out_shape=out_shape, in_specs=[pl.BlockSpec(memory...  109 us
    dot_general x1, matrix products, on_device_fast(): jnp.einsum('re,rd->ed', grad_qkv, token_rows, preferred_element_type=jnp....  29.5 us
    unnamed x183, local copies, waits for them, and re-layouts  24.4 us
    dot_general x1, matrix products, on_device_fast(): jnp.einsum('re,de->rd', grad_qkv, qkv_weight, preferred_element_type=jnp....  21.3 us
    convert_element_type x1, other arithmetic, on_device_fast(): grad_qkv_float = grad_qkv.astype(jnp.float32)  19.2 us
    reshape x4, local copies, waits for them, and re-layouts, by_row_half(): blocks = low(matrix).reshape(wide, 2, rows, half, model_width // half)  18.4 us
    convert_element_type x2, other arithmetic, on_device_fast(): grad_scores = (attention * (grad_chance - inner)).astype(jnp.bfloat16)  17.5 us
    slice x7, local copies, waits for them, and re-layouts, split_heads(): doc_block[:, which * model_width:(which + 1) * model_width]  16 us
  transfers between devices with their start and end apart: 2, of which 2 were waited for; matrix products, arithmetic and copies ran while one was open for 4% of the time, Pallas kernels for 0%

profile of v1, /device:TPU:0, one launch (start us, length us, event | category | flops | bytes accessed | tf_op | source)
XLA Modules:
  0.0 501.4 jit_solution(7628820505658888025)
XLA Ops:
  13.3 5.9 %add_convert_fusion = bf16[1024,2304]{1,0:T(8,128)(2,1)S(1)} fusion(bf16[1024,768]{1,0:T(8,128)(2,1)} %bitcast.211, bf16[768,2304]{1,0:T(8,128)(2,1)S(1)} %copy-done, f32[2304]{0:T(1024)S(1)} %maximum_convert_fusion), kind=kOutput, calls=%fused_computation.34 | convolution fusion | flops 3628597248 | bytes 9839616 | tf_op jit(solution)/shard_map/dot_general | solution.py:270
  59.5 13.7 %multiply_convert_fusion.2 = (bf16[1024,3072]{1,0:T(8,128)(2,1)S(1)}, f32[1024,3072]{1,0:T(8,128)}) fusion(f32[3072]{0:T(1024)S(1)} %copy-done.47, bf16[768,3072]{1,0:T(8,128)(2,1)} %param.31, f32[1024,768]{1,0:T(8,128)S(1)} %get-tuple-element.104, f32[768]{0:T(1024)S(1)} %copy-done.51, f32[768]{0:T(1024)S(1)} %convert_element_type.143, ...), kind=kOutput, calls=%fused_computation.22 | convolution fusion | flops 4854644736 | bytes 26765312 | tf_op jit(solution)/shard_map/dot_general | solution.py:313
  73.3 5.4 %fusion.60 = (f32[1024]{0:T(1024)S(1)}, f32[1024,768]{1,0:T(8,128)S(1)}) fusion(f32[768]{0:T(1024)S(1)} %copy-done.53, bf16[1024,3072]{1,0:T(8,128)(2,1)S(1)} %get-tuple-element.105, bf16[3072,768]{1,0:T(8,128)(2,1)S(1)} %bitcast.206, f32[768]{0:T(1024)S(1)} %copy-done.51, f32[768]{0:T(1024)S(1)} %convert_element_type.143, f32[1024]{0:T(1024)S(1)} %add_rsqrt_fusion.1, ...), kind=kOutput, calls=%fused_computation.165 | convolution fusion | flops 4837342208 | bytes 17323008 | tf_op jit(solution)/shard_map/dot_general | solution.py:318
  82.3 4.9 scatter_custom_fusion
  87.2 7.5 %all-to-all-start = ((bf16[8,32,768]{2,1,0:T(8,128)(2,1)}), bf16[8,32,768]{2,1,0:T(8,128)(2,1)}, u32[]{:S(2)}, u32[]{:S(2)}) async-start(bf16[8,32,768]{2,1,0:T(8,128)(2,1)} %bitcast.182), calls=%async_computation | async-start | bytes 786432 | tf_op jit(solution)/shard_map/all_to_all | solution.py:332
  125.0 4.8 scatter_fusion
  131.7 5.4 %all-to-all-start.1 = ((bf16[8,32,768]{2,1,0:T(8,128)(2,1)}), bf16[8,32,768]{2,1,0:T(8,128)(2,1)}, u32[]{:S(2)}, u32[]{:S(2)}) async-start(bf16[8,32,768]{2,1,0:T(8,128)(2,1)} %bitcast.183), calls=%async_computation.1 | async-start | bytes 786432 | tf_op jit(solution)/shard_map/all_to_all | solution.py:366
  148.3 8.3 %scatter_custom_fusion.3 = f32[1024,768]{1,0:T(8,128)} fusion(f32[1024,768]{1,0:T(8,128)} %bitcast_convert_fusion, s32[256]{0:T(256)} %bitcast.197, bf16[256,768]{1,0:T(8,128)(2,1)} %bitcast.24, s32[1024]{0:T(1024)} %pad_clamp_fusion), kind=kCustom, calls=%fused_computation.83 | custom fusion | flops 393216 | bytes 3543040 | tf_op jit(solution)/shard_map/scatter-add | solution.py:371
  163.3 9.7 %convolution_convert_fusion.1 = bf16[768,3072]{1,0:T(8,128)(2,1)} fusion(bf16[1024,3072]{1,0:T(8,128)(2,1)} %copy-done.70, f32[1024,768]{1,0:T(8,128)S(1)} %get-tuple-element.76), kind=kOutput, calls=%fused_computation.42 | convolution fusion | flops 4834983936 | bytes 14155776 | tf_op jit(solution)/shard_map/rd,rf->df/dot_general | solution.py:378
  173.1 11.9 %convert_reduce_fusion = (f32[3072]{0:T(1024)S(1)}, bf16[1024,3072]{1,0:T(8,128)(2,1)S(1)}) fusion(f32[1024,3072]{1,0:T(8,128)} %get-tuple-element.106, f32[3072]{0:T(1024)S(1)} %copy-done.48, bf16[3072,768]{1,0:T(8,128)(2,1)S(1)} %bitcast.208, f32[1024,768]{1,0:T(8,128)S(1)} %get-tuple-element.76), kind=kOutput, calls=%fused_computation.15 | convolution fusion | flops 4873516032 | bytes 26763264 | tf_op jit(solution)/shard_map/rd,fd->rf/dot_general | solution.py:382
  185.1 6.5 %multiply_reduce_fusion.3 = (f32[768]{0:T(1024)}, f32[1024]{0:T(1024)S(1)}, f32[1024]{0:T(1024)S(1)}, f32[768]{0:T(1024)}, f32[1024,768]{1,0:T(8,128)S(1)}) fusion(f32[1024,768]{1,0:T(8,128)S(1)} %copy-done.7, f32[1024]{0:T(1024)S(1)} %copy-done.43, f32[1024]{0:T(1024)S(1)} %copy-done.38, f32[768]{0:T(1024)S(1)} %copy-done.41, ...), kind=kOutput, calls=%fused_computation.49 | convolution fusion | flops 4839698432 | bytes 20472832 | tf_op jit(solution)/shard_map/rf,df->rd/dot_general | solution.py:391
  191.6 7.9 %convolution_convert_fusion = bf16[768,3072]{1,0:T(8,128)(2,1)} fusion(bf16[1024,3072]{1,0:T(8,128)(2,1)S(1)} %get-tuple-element.117, f32[1024,768]{1,0:T(8,128)S(1)} %copy-done.7, f32[768]{0:T(1024)S(1)} %copy-done.52, f32[768]{0:T(1024)S(1)} %copy-done.41, f32[1024]{0:T(1024)S(1)} %copy-done.43, f32[1024]{0:T(1024)S(1)} %copy-done.38), kind=kOutput, calls=%fused_computation.41 | convolution fusion | flops 4838129664 | bytes 14170112 | tf_op jit(solution)/shard_map/rd,rf->df/dot_general | solution.py:387
  210.9 6.0 %multiply_reduce_fusion.1 = (f32[12,512]{1,0:T(8,128)S(1)}, f32[12,512,512]{1,2,0:T(8,128)}) fusion(f32[12,512,512]{1,2,0:T(8,128)S(1)} %bitcast.141, f32[12,512]{1,0:T(8,128)S(1)} %copy-done.25, bf16[512,12,64]{0,2,1:T(8,128)(2,1)S(1)} %bitcast.153, bf16[512,12,64]{0,2,1:T(8,128)(2,1)S(1)} %bitcast.169), kind=kOutput, calls=%fused_computation.20 | convolution fusion | flops 412084224 | bytes 26787840 | tf_op jit(solution)/shard_map/qhd,khd->hqk/dot_general | solution.py:416
  216.9 10.6 %multiply_convert_fusion.1 = bf16[12,512,512]{1,2,0:T(8,128)(2,1)} fusion(f32[12,512,512]{1,2,0:T(8,128)} %get-tuple-element.115, f32[12,512,512]{1,2,0:T(8,128)S(1)} %bitcast.141, f32[12,512]{1,0:T(8,128)S(1)} %get-tuple-element.114, f32[12,512]{1,0:T(8,128)S(1)} %copy-done.25), kind=kLoop, calls=%fused_computation.19 | loop fusion | flops 12582912 | bytes 31506432 | tf_op jit(solution)/shard_map/convert_element_type | solution.py:420
  227.5 5.8 %multiply_convert_fusion.6 = bf16[12,64,512]{2,1,0:T(8,128)(2,1)} fusion(bf16[512,12,64]{0,2,1:T(8,128)(2,1)S(1)} %bitcast.157, bf16[12,512,512]{1,2,0:T(8,128)(2,1)} %multiply_convert_fusion.1), kind=kOutput, calls=%fused_computation.74 | convolution fusion | flops 403439616 | bytes 7864320 | tf_op jit(solution)/shard_map/hqk,qhd->khd/dot_general | solution.py:426
  240.3 6.2 %multiply_reduce_fusion = (f32[12,512]{1,0:T(8,128)S(1)}, f32[12,512,512]{1,2,0:T(8,128)}) fusion(f32[12,512,512]{1,2,0:T(8,128)S(1)} %bitcast.139, f32[12,512]{1,0:T(8,128)S(1)} %copy-done.26, bf16[512,12,64]{0,2,1:T(8,128)(2,1)S(1)} %bitcast.151, bf16[512,12,64]{0,2,1:T(8,128)(2,1)S(1)} %bitcast.167), kind=kOutput, calls=%fused_computation.17 | convolution fusion | flops 412084224 | bytes 26787840 | tf_op jit(solution)/shard_map/qhd,khd->hqk/dot_general | solution.py:416
  246.4 6.9 %multiply_convert_fusion = bf16[12,512,512]{1,2,0:T(8,128)(2,1)S(1)} fusion(f32[12,512,512]{1,2,0:T(8,128)} %get-tuple-element.113, f32[12,512,512]{1,2,0:T(8,128)S(1)} %bitcast.139, f32[12,512]{1,0:T(8,128)S(1)} %get-tuple-element.112, f32[12,512]{1,0:T(8,128)S(1)} %copy-done.26), kind=kLoop, calls=%fused_computation.16 | loop fusion | flops 12582912 | bytes 31506432 | tf_op jit(solution)/shard_map/convert_element_type | solution.py:420
  258.2 21.3 %add_convert_fusion.1 = bf16[1024,768]{1,0:T(8,128)(2,1)} fusion(f32[1024,768]{1,0:T(8,128)S(1)} %copy-done.21, bf16[768,2304]{1,0:T(8,128)(2,1)S(1)} %copy-done, bf16[512,768]{0,1:T(8,128)(2,1)S(1)} %bitcast.173, bf16[512,768]{0,1:T(8,128)(2,1)S(1)} %bitcast.179, bf16[512,768]{0,1:T(8,128)(2,1)S(1)} %bitcast.161, bf16[512,768]{0,1:T(8,128)(2,1)S(1)} %bitcast.170, ...), kind=kOutput, calls=%fused_computation.51 | convolution fusion | flops 3653763072 | bytes 12976128 | tf_op jit(solution)/shard_map/re,de->rd/dot_general | solution.py:453
  279.6 29.5 %convolution_convert_fusion.2 = bf16[2304,768]{1,0:T(8,128)(2,1)} fusion(bf16[1024,768]{1,0:T(8,128)(2,1)S(1)} %bitcast.213, bf16[512,768]{0,1:T(8,128)(2,1)S(1)} %bitcast.174, bf16[512,768]{0,1:T(8,128)(2,1)S(1)} %bitcast.180, bf16[512,768]{0,1:T(8,128)(2,1)S(1)} %bitcast.162, bf16[512,768]{0,1:T(8,128)(2,1)S(1)} %bitcast.171, ...), kind=kOutput, calls=%fused_computation.43 | convolution fusion | flops 3653959680 | bytes 9830400 | tf_op jit(solution)/shard_map/re,rd->ed/dot_general | solution.py:449
  309.1 19.2 %fusion.53 = f32[1024,2304]{0,1:T(8,128)} fusion(bf16[512,768]{0,1:T(8,128)(2,1)S(1)} %bitcast.175, bf16[512,768]{0,1:T(8,128)(2,1)} %bitcast.181, bf16[512,768]{0,1:T(8,128)(2,1)S(1)} %bitcast.163, bf16[512,768]{0,1:T(8,128)(2,1)S(1)} %bitcast.172, bf16[512,768]{0,1:T(8,128)(2,1)S(1)} %bitcast.178, bf16[512,768]{0,1:T(8,128)(2,1)S(1)} %bitcast.160), kind=kLoop, calls=%fused_computation.158 | loop fusion | flops 28311552 | bytes 14155776 | tf_op jit(solution)/shard_map/convert_element_type | solution.py:446
  328.2 9.7 %reshape.370 = bf16[8,96,4,768]{3,2,1,0:T(4,128)(2,1)} reshape(bf16[768,3072]{1,0:T(8,128)(2,1)} %convolution_convert_fusion.1) | data formatting | bytes 9437184 | tf_op jit(solution)/shard_map/reshape | solution.py:463
  338.0 5.5 %copy.80 = bf16[8,96,4,768]{3,1,2,0:T(8,128)(2,1)} copy(bf16[8,96,4,768]{3,2,1,0:T(4,128)(2,1)} %reshape.370) | data formatting | bytes 9437184 | tf_op jit(solution)/shard_map/reshape | solution.py:463
  356.1 7.9 %reshape.374 = bf16[8,2,144,2,384]{4,3,2,1,0:T(2,128)(2,1)} reshape(bf16[2304,768]{1,0:T(8,128)(2,1)} %convolution_convert_fusion.2) | data formatting | bytes 7077888 | tf_op jit(solution)/shard_map/reshape | solution.py:470
  372.6 108.8 %reduce_all.1 = (f32[96,768]{1,0:T(8,128)}, f32[192,384]{1,0:T(8,128)}, f32[2,144,384]{2,1,0:T(8,128)}, f32[2,48,384]{2,1,0:T(8,128)}, f32[176,128]{1,0:T(8,128)}) custom-call(bf16[2,2,2,2,2,96,768]{6,5,4,3,2,1,0:T(8,128)(2,1)} %bitcast.143, bf16[2,2,2,2,2,192,384]{6,5,4,3,2,1,0:T(8,128)(2,1)} %bitcast.144, bf16[2,2,2,2,2,144,384]{6,5,4,3,2,1,0:T(8,128)(2,1)} %bitcast.145, ...), custom_call_target="tpu_custom_call" | custom-call | tf_op jit(solution)/shard_map/reduce_all/pallas_call | solution.py:225
  (279 shorter events, 170.0 us)
Async XLA Ops:
  0.7 12.7 %copy-start = (bf16[768,2304]{1,0:T(8,128)(2,1)S(1)}, bf16[768,2304]{1,0:T(8,128)(2,1)}, u32[]{:S(2)}) copy-start(bf16[768,2304]{1,0:T(8,128)(2,1)} %param.24) | copy-start | bytes 10616836
  3.6 69.6 %copy-start.40 = (f32[768]{0:T(1024)}, f32[768]{0:T(1024)S(1)}, u32[]{:S(2)}) copy-start(f32[768]{0:T(1024)S(1)} %convert_element_type.143) | copy-start | bytes 9220
  10.8 68.6 %copy-start.33 = (f32[1,4,2,128]{3,1,2,0:T(4,128)}, f32[1,4,2,128]{3,1,2,0:T(4,128)S(1)}, u32[]{:S(2)}) copy-start(f32[1,4,2,128]{3,1,2,0:T(4,128)S(1)} %copy.98) | copy-start | bytes 12292
  21.4 13.8 %copy-start.59 = (pred[512]{0:T(512)(128)(4,1)S(1)}, pred[512]{0:T(512)(128)(4,1)}, u32[]{:S(2)}) copy-start(pred[512]{0:T(512)(128)(4,1)} %get-tuple-element.71) | copy-start | bytes 1540
  58.9 14.3 %copy-start.6 = (f32[1024,768]{1,0:T(8,128)}, f32[1024,768]{1,0:T(8,128)S(1)}, u32[]{:S(2)}) copy-start(f32[1024,768]{1,0:T(8,128)S(1)} %get-tuple-element.104) | copy-start | bytes 9437188
  58.9 14.3 %copy-start.37 = (f32[1024]{0:T(1024)}, f32[1024]{0:T(1024)S(1)}, u32[]{:S(2)}) copy-start(f32[1024]{0:T(1024)S(1)} %broadcast_multiply_fusion.5) | copy-start | bytes 12292
  58.9 14.3 %slice-start.6 = ((s8[4718592]{0:T(1024)(128)(4,1)}), s8[4194304]{0:T(1024)(128)(4,1)S(1)}, s32[]{:S(2)}) async-start(s8[4718592]{0:T(1024)(128)(4,1)} %bitcast.205), calls=%async_computation.8 | async-start | bytes 8388608
  59.5 13.8 %copy-start.42 = (f32[1024]{0:T(1024)}, f32[1024]{0:T(1024)S(1)}, u32[]{:S(2)}) copy-start(f32[1024]{0:T(1024)S(1)} %add_rsqrt_fusion.1) | copy-start | bytes 12292
  59.5 13.8 %copy-start.53 = (f32[768]{0:T(1024)S(1)}, f32[768]{0:T(1024)}, u32[]{:S(2)}) copy-start(f32[768]{0:T(1024)} %convert_element_type.148) | copy-start | bytes 9220
  59.5 13.8 %slice-start.7 = ((s8[4718592]{0:T(1024)(128)(4,1)}), s8[524288]{0:T(1024)(128)(4,1)S(1)}, s32[]{:S(2)}) async-start(s8[4718592]{0:T(1024)(128)(4,1)} %bitcast.205), calls=%async_computation.9 | async-start | bytes 1048576
  79.3 26.5 %copy-start.35 = (f32[1024]{0:T(1024)}, f32[1024]{0:T(1024)S(1)}, u32[]{:S(2)}) copy-start(f32[1024]{0:T(1024)S(1)} %add_rsqrt_fusion) | copy-start | bytes 12292
  87.2 19.2 %all-to-all-start = ((bf16[8,32,768]{2,1,0:T(8,128)(2,1)}), bf16[8,32,768]{2,1,0:T(8,128)(2,1)}, u32[]{:S(2)}, u32[]{:S(2)}) async-start(bf16[8,32,768]{2,1,0:T(8,128)(2,1)} %bitcast.182), calls=%async_computation | async-start | bytes 786432 | tf_op jit(solution)/shard_map/all_to_all | solution.py:332
  98.1 15.0 %copy-start.49 = (s32[256,1]{0,1:T(1,128)}, s32[256,1]{0,1:T(1,128)S(1)}, u32[]{:S(2)}) copy-start(s32[256,1]{0,1:T(1,128)S(1)} %get-tuple-element.95) | copy-start | bytes 3076
  131.7 16.6 %all-to-all-start.1 = ((bf16[8,32,768]{2,1,0:T(8,128)(2,1)}), bf16[8,32,768]{2,1,0:T(8,128)(2,1)}, u32[]{:S(2)}, u32[]{:S(2)}) async-start(bf16[8,32,768]{2,1,0:T(8,128)(2,1)} %bitcast.183), calls=%async_computation.1 | async-start | bytes 786432 | tf_op jit(solution)/shard_map/all_to_all | solution.py:366
  139.6 16.9 %copy-start.34 = (f32[1,4,2,128]{3,1,2,0:T(4,128)S(1)}, f32[1,4,2,128]{3,1,2,0:T(4,128)}, u32[]{:S(2)}) copy-start(f32[1,4,2,128]{3,1,2,0:T(4,128)} %copy-done.33) | copy-start | bytes 12292
  139.6 16.9 %copy-start.36 = (f32[1024]{0:T(1024)S(1)}, f32[1024]{0:T(1024)}, u32[]{:S(2)}) copy-start(f32[1024]{0:T(1024)} %copy-done.35) | copy-start | bytes 12292
  163.3 21.7 %slice-start.10 = ((s8[4718592]{0:T(1024)(128)(4,1)}), s8[4194304]{0:T(1024)(128)(4,1)S(1)}, s32[]{:S(2)}) async-start(s8[4718592]{0:T(1024)(128)(4,1)} %bitcast.209), calls=%async_computation.12 | async-start | bytes 8388608
  173.0 12.0 %copy-start.7 = (f32[1024,768]{1,0:T(8,128)S(1)}, f32[1024,768]{1,0:T(8,128)}, u32[]{:S(2)}) copy-start(f32[1024,768]{1,0:T(8,128)} %copy-done.6) | copy-start | bytes 9437188
  173.0 12.0 %copy-start.38 = (f32[1024]{0:T(1024)S(1)}, f32[1024]{0:T(1024)}, u32[]{:S(2)}) copy-start(f32[1024]{0:T(1024)} %copy-done.37) | copy-start | bytes 12292
  216.9 20.4 %slice-start = ((s8[12582912]{0:T(1024)(128)(4,1)}), s8[4194304]{0:T(1024)(128)(4,1)S(1)}, s32[]{:S(2)}) async-start(s8[12582912]{0:T(1024)(128)(4,1)} %bitcast.138), calls=%async_computation.2 | async-start | bytes 8388608
  216.9 20.4 %slice-start.1 = ((s8[12582912]{0:T(1024)(128)(4,1)}), s8[4194304]{0:T(1024)(128)(4,1)S(1)}, s32[]{:S(2)}) async-start(s8[12582912]{0:T(1024)(128)(4,1)} %bitcast.138), calls=%async_computation.3 | async-start | bytes 8388608
  255.4 24.2 %copy-start.24 = (bf16[12,64,512]{2,1,0:T(8,128)(2,1)}, bf16[12,64,512]{2,1,0:T(8,128)(2,1)S(1)}, u32[]{:S(2)}) copy-start(bf16[12,64,512]{2,1,0:T(8,128)(2,1)S(1)} %multiply_convert_fusion.4) | copy-start | bytes 2359300
  258.2 21.3 %copy-start.63 = (bf16[2,512,768]{2,1,0:T(8,128)(2,1)S(1)}, bf16[2,512,768]{2,1,0:T(8,128)(2,1)}, u32[]{:S(2)}) copy-start(bf16[2,512,768]{2,1,0:T(8,128)(2,1)} %param.22) | copy-start | bytes 4718596
  279.6 29.5 %copy-start.23 = (bf16[12,64,512]{2,1,0:T(8,128)(2,1)S(1)}, bf16[12,64,512]{2,1,0:T(8,128)(2,1)}, u32[]{:S(2)}) copy-start(bf16[12,64,512]{2,1,0:T(8,128)(2,1)} %multiply_convert_fusion.6) | copy-start | bytes 2359300
  (61 other events, 292.1 us)
